TPU v7x, 256 devices: a whole 4x4x8 slice. The times are simulated.
256 devices in a mesh: grp: 8 (over y, core), sub: 32 (over z, x).
Axes of the slice: x: 4, y: 4, z: 8, core: 2. Of those that a mesh axis runs over, the one named last changes fastest.
Arguments:
- schur_block: float32 [8, 32, 1152, 1152], P('grp', 'sub')
- dirichlet_inverse: float32 [8, 32, 1152, 1152], P('grp', 'sub')
- coarse_basis: float32 [8, 32, 24, 1152], P('grp', 'sub'), may hold values from -0.3125 to 0.3125
- coarse_inverse: float32 [8, 768, 768], P('grp', None, 'sub')
- coarse_owner: int32 [8, 768], P('grp', 'sub'), may hold values from 0 to 767, each once within a row
- face_count: int32 [8, 32, 4], P('grp', 'sub'), may hold values from 0 to 384, as said below
- face_rows: int32 [8, 32, 4, 384], P('grp', 'sub'), may hold values from 0 to 1151, as said below
- multiplicity: int32 [8, 32, 1152], P('grp', 'sub'), may hold values from 1 to 5, as said below
- gradient: float32 [8, 32, 192, 1152], P('grp', 'sub'), may hold values from -6 to 6
- warm_start: float32 [8, 32, 192, 1152], P('grp', 'sub'), may hold values from -3 to 3
Outputs:
- adjoint: float32 [8, 32, 192, 1152], P('grp', 'sub')
Inputs may be any that keep to these rules, and one draw needn't show every extreme that they name: `coarse_owner`: each group's row names each coarse unknown once. `face_count`: faces across one grp or sub step have equal counts on both sides; faces 2 and 3 at the ends of sub have count 0; some face has count 384 in every draw. `face_rows`: the live entries of one face are distinct rows; entry k of a face and entry k of the matching face of the neighbour name the same unknown; a row may lie on several faces. `multiplicity`: one plus the number of live face entries that name the row.
All inputs are finite; a program needn't handle non-finite values.
Results may differ from a plain program's by a relative error of at most 0.00023.
Values sent between devices are 32-bit elements; how exact they have to be, the bound alone decides.
A program may use at most 128 MiB of HBM per device.

v0:
```python
import jax
import jax.numpy as jnp
from jax import lax
from jax.sharding import PartitionSpec as P

ITERS = 3
HIGHEST = lax.Precision.HIGHEST


def shifted(array, axis, by):
    peers = lax.axis_size(axis)
    return lax.ppermute(array, axis, [(i, (i + by) % peers) for i in range(peers)])


def from_behind(value, axis, steps):
    count = lax.axis_size(axis)
    first, last = (max(0, -steps), min(count, count - steps))
    return lax.ppermute(value, axis, [(source, source + steps) for source in range(first, last)])


def product(left, right):
    return jnp.dot(left, right, precision=HIGHEST, preferred_element_type=jnp.float32)


def local(
    schur_block,
    dirichlet_inverse,
    coarse_basis,
    coarse_inverse,
    coarse_owner,
    face_count,
    face_rows,
    multiplicity,
    gradient,
    warm_start,
):
    schur_local = schur_block[0, 0]
    dirichlet_local = dirichlet_inverse[0, 0]
    coarse_rows = coarse_basis[0, 0]
    face_index = face_rows[0, 0]
    live_mask = (jnp.arange(face_index.shape[1])[None, :] < face_count[0, 0][:, None]).astype(
        jnp.float32
    )
    weight = (1.0 / multiplicity[0, 0].astype(jnp.float32))[None, :]
    my_owner = coarse_owner[0]
    all_owner = lax.all_gather(coarse_owner, "sub", axis=1, tiled=True)[0]

    def assemble(values):
        outgoing = jax.vmap(lambda one_index, one_mask: values[:, one_index] * one_mask[None, :])(
            face_index, live_mask
        )
        from_next = shifted(outgoing[1], "grp", -1)
        from_prev = shifted(outgoing[0], "grp", 1)
        from_after = from_behind(outgoing[3], "sub", -1)
        from_before = from_behind(outgoing[2], "sub", 1)
        values = values.at[:, face_index[0]].add(from_next)
        values = values.at[:, face_index[1]].add(from_prev)
        values = values.at[:, face_index[2]].add(from_after)
        return values.at[:, face_index[3]].add(from_before)

    adjoint = warm_start[0, 0]
    right_side = gradient[0, 0]
    for iteration in range(ITERS):
        applied = product(adjoint, schur_local)
        residual = right_side - assemble(applied)
        weighted = residual * weight
        local_part = product(weighted, dirichlet_local)
        coarse_piece = lax.dot_general(
            weighted,
            coarse_rows,
            (((1,), (1,)), ((), ())),
            precision=HIGHEST,
            preferred_element_type=jnp.float32,
        )
        pieces = lax.all_gather(coarse_piece, "sub", axis=1, tiled=True)
        coarse_sum = jnp.zeros_like(pieces).at[:, all_owner].set(pieces)
        owned = product(coarse_sum, coarse_inverse[0])
        gathered = lax.all_gather(owned, "sub", axis=1, tiled=True)
        picked = gathered[:, my_owner]
        correction = product(picked, coarse_rows)
        adjoint = adjoint + assemble((local_part + correction) * weight)
    return adjoint[None, None]


def solution(mesh):
    in_specs = (
        P("grp", "sub", None, None),
        P("grp", "sub", None, None),
        P("grp", "sub", None, None),
        P("grp", None, "sub"),
        P("grp", "sub"),
        P("grp", "sub", None),
        P("grp", "sub", None, None),
        P("grp", "sub", None),
        P("grp", "sub", None, None),
        P("grp", "sub", None, None),
    )
    out_specs = P("grp", "sub", None, None)
    return jax.shard_map(local, mesh=mesh, in_specs=in_specs, out_specs=out_specs, check_vma=False)
```

profile of v0, /device:TPU:1, one launch (start us, length us, event | category | flops | bytes accessed | tf_op | source)
XLA Modules:
  0.0 631.9 jit_solution(7648857142585618406)
XLA Ops:
  1.5 11.3 %fusion.10 = f32[192,1152]{0,1:T(8,128)S(1)} fusion(f32[1,1,1152,1152]{3,2,1,0:T(8,128)} %param.10, f32[1,1,192,1152]{3,2,1,0:T(8,128)} %param.19), kind=kOutput, calls=%fused_computation.46 | convolution fusion | flops 3057647616 | bytes 7077888 | tf_op jit(solution)/shard_map/dot_general | solution.py:22
  12.8 4.7 gather_fusion
  28.1 22.5 %all-reduce = s32[768]{0:T(1024)S(1)} all-reduce(s32[768]{0:T(1024)S(1)} %bitcast_dynamic-update-slice_fusion), channel_id=1, replica_groups=mesh['grp'=8,'sub'=32] {'sub'}, use_global_device_ids=true, to_apply=%add | all-reduce | flops 768 | bytes 6144
  66.9 36.0 %all_gather.22 = f32[192,768]{0,1:T(8,128)S(1)} all-gather(f32[192,24]{0,1:T(8,128)S(1)} %fusion.97), channel_id=1, replica_groups=mesh['grp'=8,'sub'=32] {'sub'}, dimensions={1}, use_global_device_ids=true | all-gather | bytes 608256 | tf_op jit(solution)/shard_map/all_gather | solution.py:75
  102.9 6.3 scatter_custom_fusion.4
  110.9 41.2 %all_gather.23 = f32[192,768]{0,1:T(8,128)} all-gather(f32[192,24]{0,1:T(8,128)S(1)} %fusion.113), channel_id=1, replica_groups=mesh['grp'=8,'sub'=32] {'sub'}, dimensions={1}, use_global_device_ids=true | all-gather | bytes 608256 | tf_op jit(solution)/shard_map/all_gather | solution.py:78
  154.7 8.0 %bitcast_add_fusion = (f32[192,1152]{1,0:T(8,128)}, f32[192,1152]{1,0:T(8,128)}) fusion(f32[1,1,192,1152]{3,2,1,0:T(8,128)S(1)} %copy-done.6, f32[1152]{0:T(1024)S(1)} %divide_reduce_fusion, f32[192,1152]{1,0:T(8,128)S(1)} %fusion.106, f32[1,1,1152,1152]{3,2,1,0:T(8,128)} %param.11, f32[192,1152]{1,0:T(8,128)S(1)} %copy.31, ...), kind=kOutput, calls=%fused_computation.66 | convolution fusion | flops 3058753536 | bytes 10621440 | tf_op jit(solution)/shard_map/dot_general | solution.py:22
  164.2 4.7 gather_fusion.2
  171.8 28.8 %collective-permute-start.4 = (f32[192,384]{0,1:T(8,128)}, f32[192,384]{0,1:T(8,128)}, u32[]{:S(2)}, u32[]{:S(2)}) collective-permute-start(f32[192,384]{0,1:T(8,128)} %get-tuple-element.28), channel_id=1, source_target_pairs={{0,224},{32,0},{64,32},{96,64},{128,96},{160,128},{192,160},{224,1... | collective-permute-start | bytes 884744 | tf_op jit(solution)/shard_map/ppermute | solution.py:12
  203.0 4.7 collective-permute-start.7
  218.9 4.0 scatter_custom_fusion.8
  222.9 11.1 %fusion.8 = f32[192,1152]{0,1:T(8,128)S(1)} fusion(f32[192,1152]{0,1:T(8,128)S(1)} %scatter_custom_fusion.8, f32[1,1,1152,1152]{3,2,1,0:T(8,128)} %param.10), kind=kOutput, calls=%fused_computation.44 | convolution fusion | flops 3057647616 | bytes 7077888 | tf_op jit(solution)/shard_map/dot_general | solution.py:22
  234.0 4.7 gather_fusion.3
  244.4 4.8 collective-permute-start.11
  267.1 39.6 %all_gather.24 = f32[192,768]{0,1:T(8,128)S(1)} all-gather(f32[192,24]{0,1:T(8,128)S(1)} %fusion.94), channel_id=1, replica_groups=mesh['grp'=8,'sub'=32] {'sub'}, dimensions={1}, use_global_device_ids=true | all-gather | bytes 608256 | tf_op jit(solution)/shard_map/all_gather | solution.py:75
  306.6 6.3 scatter_custom_fusion.13
  314.6 42.3 %all_gather.25 = f32[192,768]{0,1:T(8,128)} all-gather(f32[192,24]{0,1:T(8,128)S(1)} %fusion.111), channel_id=1, replica_groups=mesh['grp'=8,'sub'=32] {'sub'}, dimensions={1}, use_global_device_ids=true | all-gather | bytes 608256 | tf_op jit(solution)/shard_map/all_gather | solution.py:78
  359.6 7.7 %fusion.24 = f32[192,1152]{1,0:T(8,128)} fusion(f32[192,1152]{1,0:T(8,128)S(1)} %fusion.103, f32[1,1,1152,1152]{3,2,1,0:T(8,128)} %param.11, f32[1152]{0:T(1024)S(1)} %divide_reduce_fusion, f32[192,1152]{1,0:T(8,128)S(1)} %copy-done.3, f32[1,1,192,1152]{3,2,1,0:T(8,128)S(1)} %copy-done.1), kind=kOutput, calls=%fused_computation.52 | convolution fusion | flops 3058532352 | bytes 8851968 | tf_op jit(solution)/shard_map/dot_general | solution.py:22
  368.8 4.7 gather_fusion.5
  376.3 24.3 %collective-permute-start.12 = (f32[192,384]{0,1:T(8,128)}, f32[192,384]{0,1:T(8,128)}, u32[]{:S(2)}, u32[]{:S(2)}) collective-permute-start(f32[192,384]{0,1:T(8,128)} %get-tuple-element.20), channel_id=1, source_target_pairs={{0,224},{32,0},{64,32},{96,64},{128,96},{160,128},{192,160},{224,1... | collective-permute-start | bytes 884744 | tf_op jit(solution)/shard_map/ppermute | solution.py:12
  402.7 4.7 collective-permute-start.15
  423.2 4.0 scatter_custom_fusion.17
  427.2 11.1 %fusion.6 = f32[192,1152]{0,1:T(8,128)S(1)} fusion(f32[192,1152]{0,1:T(8,128)S(1)} %scatter_custom_fusion.17, f32[1,1,1152,1152]{3,2,1,0:T(8,128)} %param.10), kind=kOutput, calls=%fused_computation.42 | convolution fusion | flops 3057647616 | bytes 7077888 | tf_op jit(solution)/shard_map/dot_general | solution.py:22
  438.3 4.7 gather_fusion.6
  448.7 4.8 collective-permute-start.19
  471.3 40.6 %all_gather.26 = f32[192,768]{0,1:T(8,128)S(1)} all-gather(f32[192,24]{0,1:T(8,128)S(1)} %fusion.91), channel_id=1, replica_groups=mesh['grp'=8,'sub'=32] {'sub'}, dimensions={1}, use_global_device_ids=true | all-gather | bytes 608256 | tf_op jit(solution)/shard_map/all_gather | solution.py:75
  511.9 6.3 scatter_custom_fusion.22
  519.9 42.2 %all_gather.27 = f32[192,768]{0,1:T(8,128)} all-gather(f32[192,24]{0,1:T(8,128)S(1)} %fusion.109), channel_id=1, replica_groups=mesh['grp'=8,'sub'=32] {'sub'}, dimensions={1}, use_global_device_ids=true | all-gather | bytes 608256 | tf_op jit(solution)/shard_map/all_gather | solution.py:78
  564.8 7.7 %fusion.21 = f32[192,1152]{1,0:T(8,128)} fusion(f32[192,1152]{1,0:T(8,128)S(1)} %fusion.100, f32[1,1,1152,1152]{3,2,1,0:T(8,128)} %param.11, f32[1152]{0:T(1024)S(1)} %divide_reduce_fusion, f32[192,1152]{1,0:T(8,128)S(1)} %copy-done.2, f32[1,1,192,1152]{3,2,1,0:T(8,128)S(1)} %copy-done.1), kind=kOutput, calls=%fused_computation.51 | convolution fusion | flops 3058532352 | bytes 8851968 | tf_op jit(solution)/shard_map/dot_general | solution.py:22
  574.0 4.7 gather_fusion.8
  581.3 24.9 %collective-permute-start.20 = (f32[192,384]{0,1:T(8,128)}, f32[192,384]{0,1:T(8,128)}, u32[]{:S(2)}, u32[]{:S(2)}) collective-permute-start(f32[192,384]{0,1:T(8,128)} %get-tuple-element.12), channel_id=1, source_target_pairs={{0,224},{32,0},{64,32},{96,64},{128,96},{160,128},{192,160},{224,1... | collective-permute-start | bytes 884744 | tf_op jit(solution)/shard_map/ppermute | solution.py:12
  608.0 4.7 collective-permute-start.23
  (138 shorter events, 152.0 us)
Async XLA Ops:
  0.0 65.2 %copy-start = (f32[1,1,24,1152]{3,2,1,0:T(8,128)S(1)}, f32[1,1,24,1152]{3,2,1,0:T(8,128)}, u32[]{:S(2)}) copy-start(f32[1,1,24,1152]{3,2,1,0:T(8,128)} %param.12) | copy-start | bytes 331780
  19.3 42.3 %collective-permute-start.3 = (f32[192,384]{0,1:T(8,128)S(1)}, f32[192,384]{0,1:T(8,128)S(1)}, u32[]{:S(2)}, u32[]{:S(2)}) collective-permute-start(f32[192,384]{0,1:T(8,128)S(1)} %get-tuple-element.29), channel_id=1, source_target_pairs={{0,1},{1,2},{2,3},{3,4},{4,5},{5,6},{6,7},{7,8},{8,9},{9,10},{10,1... | collective-permute-start | bytes 884744 | tf_op jit(solution)/shard_map/ppermute | solution.py:18
  23.3 34.8 %collective-permute-start.2 = (f32[192,384]{0,1:T(8,128)S(1)}, f32[192,384]{0,1:T(8,128)}, u32[]{:S(2)}, u32[]{:S(2)}) collective-permute-start(f32[192,384]{0,1:T(8,128)S(1)} %get-tuple-element.30), channel_id=1, source_target_pairs={{1,0},{2,1},{3,2},{4,3},{5,4},{6,5},{7,6},{8,7},{9,8},{10,9},{11,1... | collective-permute-start | bytes 884744 | tf_op jit(solution)/shard_map/ppermute | solution.py:18
  24.6 29.7 %collective-permute-start.1 = (f32[192,384]{0,1:T(8,128)S(1)}, f32[192,384]{0,1:T(8,128)}, u32[]{:S(2)}, u32[]{:S(2)}) collective-permute-start(f32[192,384]{0,1:T(8,128)S(1)} %get-tuple-element.31), channel_id=1, source_target_pairs={{0,32},{32,64},{64,96},{96,128},{128,160},{160,192},{192,224},{224... | collective-permute-start | bytes 884744 | tf_op jit(solution)/shard_map/ppermute | solution.py:12
  26.7 24.0 %collective-permute-start = (f32[192,384]{0,1:T(8,128)S(1)}, f32[192,384]{0,1:T(8,128)}, u32[]{:S(2)}, u32[]{:S(2)}) collective-permute-start(f32[192,384]{0,1:T(8,128)S(1)} %get-tuple-element.32), channel_id=1, source_target_pairs={{0,224},{32,0},{64,32},{96,64},{128,96},{160,128},{192,160},{224,1... | collective-permute-start | bytes 884744 | tf_op jit(solution)/shard_map/ppermute | solution.py:12
  66.9 42.4 %copy-start.8 = (f32[1,768,24]{1,2,0:T(8,128)S(1)}, f32[1,768,24]{1,2,0:T(8,128)}, u32[]{:S(2)}) copy-start(f32[1,768,24]{1,2,0:T(8,128)} %param.13) | copy-start | bytes 221188
  110.8 43.8 %copy-start.6 = (f32[1,1,192,1152]{3,2,1,0:T(8,128)S(1)}, f32[1,1,192,1152]{3,2,1,0:T(8,128)}, u32[]{:S(2)}) copy-start(f32[1,1,192,1152]{3,2,1,0:T(8,128)} %param.19) | copy-start | bytes 2654212
  170.6 37.2 %copy-start.7 = (f32[192,1152]{1,0:T(8,128)S(1)}, f32[192,1152]{1,0:T(8,128)}, u32[]{:S(2)}) copy-start(f32[192,1152]{1,0:T(8,128)} %get-tuple-element.33) | copy-start | bytes 2654212
  171.8 36.4 %collective-permute-start.4 = (f32[192,384]{0,1:T(8,128)}, f32[192,384]{0,1:T(8,128)}, u32[]{:S(2)}, u32[]{:S(2)}) collective-permute-start(f32[192,384]{0,1:T(8,128)} %get-tuple-element.28), channel_id=1, source_target_pairs={{0,224},{32,0},{64,32},{96,64},{128,96},{160,128},{192,160},{224,1... | collective-permute-start | bytes 884744 | tf_op jit(solution)/shard_map/ppermute | solution.py:12
  200.6 11.1 %collective-permute-start.5 = (f32[192,384]{0,1:T(8,128)}, f32[192,384]{0,1:T(8,128)}, u32[]{:S(2)}, u32[]{:S(2)}) collective-permute-start(f32[192,384]{0,1:T(8,128)} %get-tuple-element.27), channel_id=1, source_target_pairs={{0,32},{32,64},{64,96},{96,128},{128,160},{160,192},{192,224},{224... | collective-permute-start | bytes 884744 | tf_op jit(solution)/shard_map/ppermute | solution.py:12
  201.7 13.6 %collective-permute-start.6 = (f32[192,384]{0,1:T(8,128)}, f32[192,384]{0,1:T(8,128)}, u32[]{:S(2)}, u32[]{:S(2)}) collective-permute-start(f32[192,384]{0,1:T(8,128)} %get-tuple-element.26), channel_id=1, source_target_pairs={{1,0},{2,1},{3,2},{4,3},{5,4},{6,5},{7,6},{8,7},{9,8},{10,9},{11,1... | collective-permute-start | bytes 884744 | tf_op jit(solution)/shard_map/ppermute | solution.py:18
  203.0 15.9 %collective-permute-start.7 = (f32[192,384]{0,1:T(8,128)}, f32[192,384]{0,1:T(8,128)}, u32[]{:S(2)}, u32[]{:S(2)}) collective-permute-start(f32[192,384]{0,1:T(8,128)} %get-tuple-element.25), channel_id=1, source_target_pairs={{0,1},{1,2},{2,3},{3,4},{4,5},{5,6},{6,7},{7,8},{8,9},{9,10},{10,1... | collective-permute-start | bytes 884744 | tf_op jit(solution)/shard_map/ppermute | solution.py:18
  241.4 7.8 %collective-permute-start.8 = (f32[192,384]{0,1:T(8,128)S(1)}, f32[192,384]{0,1:T(8,128)}, u32[]{:S(2)}, u32[]{:S(2)}) collective-permute-start(f32[192,384]{0,1:T(8,128)S(1)} %get-tuple-element.24), channel_id=1, source_target_pairs={{0,224},{32,0},{64,32},{96,64},{128,96},{160,128},{192,160},{224,1... | collective-permute-start | bytes 884744 | tf_op jit(solution)/shard_map/ppermute | solution.py:12
  241.4 11.4 %collective-permute-start.9 = (f32[192,384]{0,1:T(8,128)}, f32[192,384]{0,1:T(8,128)}, u32[]{:S(2)}, u32[]{:S(2)}) collective-permute-start(f32[192,384]{0,1:T(8,128)} %get-tuple-element.23), channel_id=1, source_target_pairs={{0,32},{32,64},{64,96},{96,128},{128,160},{160,192},{192,224},{224... | collective-permute-start | bytes 884744 | tf_op jit(solution)/shard_map/ppermute | solution.py:12
  243.1 13.4 %collective-permute-start.10 = (f32[192,384]{0,1:T(8,128)}, f32[192,384]{0,1:T(8,128)}, u32[]{:S(2)}, u32[]{:S(2)}) collective-permute-start(f32[192,384]{0,1:T(8,128)} %get-tuple-element.22), channel_id=1, source_target_pairs={{1,0},{2,1},{3,2},{4,3},{5,4},{6,5},{7,6},{8,7},{9,8},{10,9},{11,1... | collective-permute-start | bytes 884744 | tf_op jit(solution)/shard_map/ppermute | solution.py:18
  244.4 15.7 %collective-permute-start.11 = (f32[192,384]{0,1:T(8,128)}, f32[192,384]{0,1:T(8,128)}, u32[]{:S(2)}, u32[]{:S(2)}) collective-permute-start(f32[192,384]{0,1:T(8,128)} %get-tuple-element.21), channel_id=1, source_target_pairs={{0,1},{1,2},{2,3},{3,4},{4,5},{5,6},{6,7},{7,8},{8,9},{9,10},{10,1... | collective-permute-start | bytes 884744 | tf_op jit(solution)/shard_map/ppermute | solution.py:18
  314.6 45.0 %copy-start.3 = (f32[192,1152]{1,0:T(8,128)S(1)}, f32[192,1152]{1,0:T(8,128)}, u32[]{:S(2)}) copy-start(f32[192,1152]{1,0:T(8,128)} %copy.36) | copy-start | bytes 2654212
  376.3 32.4 %copy-start.5 = (f32[192,1152]{1,0:T(8,128)S(1)}, f32[192,1152]{1,0:T(8,128)}, u32[]{:S(2)}) copy-start(f32[192,1152]{1,0:T(8,128)} %fusion.24) | copy-start | bytes 2654212
  376.3 36.1 %collective-permute-start.12 = (f32[192,384]{0,1:T(8,128)}, f32[192,384]{0,1:T(8,128)}, u32[]{:S(2)}, u32[]{:S(2)}) collective-permute-start(f32[192,384]{0,1:T(8,128)} %get-tuple-element.20), channel_id=1, source_target_pairs={{0,224},{32,0},{64,32},{96,64},{128,96},{160,128},{192,160},{224,1... | collective-permute-start | bytes 884744 | tf_op jit(solution)/shard_map/ppermute | solution.py:12
  400.6 15.4 %collective-permute-start.13 = (f32[192,384]{0,1:T(8,128)}, f32[192,384]{0,1:T(8,128)}, u32[]{:S(2)}, u32[]{:S(2)}) collective-permute-start(f32[192,384]{0,1:T(8,128)} %get-tuple-element.19), channel_id=1, source_target_pairs={{0,32},{32,64},{64,96},{96,128},{128,160},{160,192},{192,224},{224... | collective-permute-start | bytes 884744 | tf_op jit(solution)/shard_map/ppermute | solution.py:12
  401.4 18.2 %collective-permute-start.14 = (f32[192,384]{0,1:T(8,128)}, f32[192,384]{0,1:T(8,128)}, u32[]{:S(2)}, u32[]{:S(2)}) collective-permute-start(f32[192,384]{0,1:T(8,128)} %get-tuple-element.18), channel_id=1, source_target_pairs={{1,0},{2,1},{3,2},{4,3},{5,4},{6,5},{7,6},{8,7},{9,8},{10,9},{11,1... | collective-permute-start | bytes 884744 | tf_op jit(solution)/shard_map/ppermute | solution.py:18
  402.7 20.5 %collective-permute-start.15 = (f32[192,384]{0,1:T(8,128)}, f32[192,384]{0,1:T(8,128)}, u32[]{:S(2)}, u32[]{:S(2)}) collective-permute-start(f32[192,384]{0,1:T(8,128)} %get-tuple-element.17), channel_id=1, source_target_pairs={{0,1},{1,2},{2,3},{3,4},{4,5},{5,6},{6,7},{7,8},{8,9},{9,10},{10,1... | collective-permute-start | bytes 884744 | tf_op jit(solution)/shard_map/ppermute | solution.py:18
  445.7 7.8 %collective-permute-start.16 = (f32[192,384]{0,1:T(8,128)S(1)}, f32[192,384]{0,1:T(8,128)}, u32[]{:S(2)}, u32[]{:S(2)}) collective-permute-start(f32[192,384]{0,1:T(8,128)S(1)} %get-tuple-element.16), channel_id=1, source_target_pairs={{0,224},{32,0},{64,32},{96,64},{128,96},{160,128},{192,160},{224,1... | collective-permute-start | bytes 884744 | tf_op jit(solution)/shard_map/ppermute | solution.py:12
  446.0 11.0 %collective-permute-start.17 = (f32[192,384]{0,1:T(8,128)}, f32[192,384]{0,1:T(8,128)}, u32[]{:S(2)}, u32[]{:S(2)}) collective-permute-start(f32[192,384]{0,1:T(8,128)} %get-tuple-element.15), channel_id=1, source_target_pairs={{0,32},{32,64},{64,96},{96,128},{128,160},{160,192},{192,224},{224... | collective-permute-start | bytes 884744 | tf_op jit(solution)/shard_map/ppermute | solution.py:12
  447.4 13.4 %collective-permute-start.18 = (f32[192,384]{0,1:T(8,128)}, f32[192,384]{0,1:T(8,128)}, u32[]{:S(2)}, u32[]{:S(2)}) collective-permute-start(f32[192,384]{0,1:T(8,128)} %get-tuple-element.14), channel_id=1, source_target_pairs={{1,0},{2,1},{3,2},{4,3},{5,4},{6,5},{7,6},{8,7},{9,8},{10,9},{11,1... | collective-permute-start | bytes 884744 | tf_op jit(solution)/shard_map/ppermute | solution.py:18
  448.7 15.7 %collective-permute-start.19 = (f32[192,384]{0,1:T(8,128)}, f32[192,384]{0,1:T(8,128)}, u32[]{:S(2)}, u32[]{:S(2)}) collective-permute-start(f32[192,384]{0,1:T(8,128)} %get-tuple-element.13), channel_id=1, source_target_pairs={{0,1},{1,2},{2,3},{3,4},{4,5},{5,6},{6,7},{7,8},{8,9},{9,10},{10,1... | collective-permute-start | bytes 884744 | tf_op jit(solution)/shard_map/ppermute | solution.py:18
  519.9 44.9 %copy-start.2 = (f32[192,1152]{1,0:T(8,128)S(1)}, f32[192,1152]{1,0:T(8,128)}, u32[]{:S(2)}) copy-start(f32[192,1152]{1,0:T(8,128)} %copy.42) | copy-start | bytes 2654212
  581.3 31.7 %copy-start.4 = (f32[192,1152]{1,0:T(8,128)S(1)}, f32[192,1152]{1,0:T(8,128)}, u32[]{:S(2)}) copy-start(f32[192,1152]{1,0:T(8,128)} %fusion.21) | copy-start | bytes 2654212
  581.3 34.3 %collective-permute-start.20 = (f32[192,384]{0,1:T(8,128)}, f32[192,384]{0,1:T(8,128)}, u32[]{:S(2)}, u32[]{:S(2)}) collective-permute-start(f32[192,384]{0,1:T(8,128)} %get-tuple-element.12), channel_id=1, source_target_pairs={{0,224},{32,0},{64,32},{96,64},{128,96},{160,128},{192,160},{224,1... | collective-permute-start | bytes 884744 | tf_op jit(solution)/shard_map/ppermute | solution.py:12
  606.2 13.0 %collective-permute-start.21 = (f32[192,384]{0,1:T(8,128)}, f32[192,384]{0,1:T(8,128)}, u32[]{:S(2)}, u32[]{:S(2)}) collective-permute-start(f32[192,384]{0,1:T(8,128)} %get-tuple-element.11), channel_id=1, source_target_pairs={{0,32},{32,64},{64,96},{96,128},{128,160},{160,192},{192,224},{224... | collective-permute-start | bytes 884744 | tf_op jit(solution)/shard_map/ppermute | solution.py:12
  606.7 16.1 %collective-permute-start.22 = (f32[192,384]{0,1:T(8,128)}, f32[192,384]{0,1:T(8,128)}, u32[]{:S(2)}, u32[]{:S(2)}) collective-permute-start(f32[192,384]{0,1:T(8,128)} %get-tuple-element.10), channel_id=1, source_target_pairs={{1,0},{2,1},{3,2},{4,3},{5,4},{6,5},{7,6},{8,7},{9,8},{10,9},{11,1... | collective-permute-start | bytes 884744 | tf_op jit(solution)/shard_map/ppermute | solution.py:18
  608.0 18.6 %collective-permute-start.23 = (f32[192,384]{0,1:T(8,128)S(1)}, f32[192,384]{0,1:T(8,128)}, u32[]{:S(2)}, u32[]{:S(2)}) collective-permute-start(f32[192,384]{0,1:T(8,128)S(1)} %get-tuple-element.9), channel_id=1, source_target_pairs={{0,1},{1,2},{2,3},{3,4},{4,5},{5,6},{6,7},{7,8},{8,9},{9,10},{10,1... | collective-permute-start | bytes 884744 | tf_op jit(solution)/shard_map/ppermute | solution.py:18
  (5 other events, 79.3 us)
where the time goes:
time: 643 us; the launch traced here: 632 us
  blocking collectives  264 us (41%)
  starting transfers between devices  121 us (19%)
  other arithmetic  101 us (16%)
  local copies, waits for them, and re-layouts  73 us (11%)
  matrix products  69.6 us (11%)
    all_gather x3, blocking collectives, local(): gathered = lax.all_gather(owned, 'sub', axis=1, tiled=True)  126 us
    all_gather x3, blocking collectives, local(): pieces = lax.all_gather(coarse_piece, 'sub', axis=1, tiled=True)  116 us
    ppermute x12, starting transfers between devices, shifted(): lax.ppermute(array, axis, [(i, (i + by) % peers) for i in range(peers)])  86.1 us
    dot_general x12, matrix products, product(): jnp.dot(left, right, precision=HIGHEST, preferred_element_type=jnp.float32)  64.5 us
    ppermute x12, starting transfers between devices, from_behind(): lax.ppermute(value, axis, [(source, source + steps) for source in range(f...  35.4 us
    gather x6, local copies, waits for them, and re-layouts, assemble(): values[:, one_index] * one_mask[None, :]  27.9 us
    unnamed x1, blocking collectives  22.5 us
    scatter-add x6, other arithmetic, assemble(): values = values.at[:, face_index[1]].add(from_prev)  21.9 us
  transfers between devices with their start and end apart: 24, of which 0 were waited for; matrix products, arithmetic and copies ran while one was open for 12% of the time, Pallas kernels for 0%

commit v1 on v0

--- a/solution.py
+++ b/solution.py
@@ -72,7 +72,8 @@
             precision=HIGHEST,
             preferred_element_type=jnp.float32,
         )
-        pieces = lax.all_gather(coarse_piece, "sub", axis=1, tiled=True)
+        copies = jnp.concatenate([coarse_piece] * lax.axis_size("sub"), axis=1)
+        pieces = lax.all_to_all(copies, "sub", 1, 1, tiled=True)
         coarse_sum = jnp.zeros_like(pieces).at[:, all_owner].set(pieces)
         owned = product(coarse_sum, coarse_inverse[0])
         gathered = lax.all_gather(owned, "sub", axis=1, tiled=True)

time: 643 us -> 584 us (0.908)
  blocking collectives: 264 us -> 206 us
  local copies, waits for them, and re-layouts: 73 us -> 91.5 us
  starting transfers between devices: 121 us -> 105 us
    all_gather x3 -> x0, blocking collectives: 116 us -> none  [local(): pieces = lax.all_gather(coarse_piece, 'sub', axis=1, tiled=True)]
    all_to_all x0 -> x2, blocking collectives: none -> 60.7 us  [local(): pieces = lax.all_to_all(copies, 'sub', 1, 1, tiled=True)]
    ppermute x12, starting transfers between devices: 86.1 us -> 57.3 us  [shifted(): lax.ppermute(array, axis, [(i, (i + by) % peers) for i in range(peers)])]
    unnamed x29 -> x145, local copies, waits for them, and re-layouts: 1.57 us -> 20.9 us
    all_to_all x0 -> x1, starting transfers between devices: none -> 12.5 us  [local(): pieces = lax.all_to_all(copies, 'sub', 1, 1, tiled=True)]
  transfers between devices with their start and end apart: 24 -> 25, of which waited for: 0 -> 0; matrix products, arithmetic and copies ran while one was open for 12% -> 13% of each run, Pallas kernels for 0% -> 0%
where the time goes in v1:
time: 584 us; the launch traced here: 574 us
  blocking collectives  206 us (35%)
  starting transfers between devices  105 us (18%)
  other arithmetic  101 us (17%)
  local copies, waits for them, and re-layouts  91.5 us (16%)
  matrix products  67.6 us (12%)
    all_gather x3, blocking collectives, local(): gathered = lax.all_gather(owned, 'sub', axis=1, tiled=True)  122 us
    dot_general x12, matrix products, product(): jnp.dot(left, right, precision=HIGHEST, preferred_element_type=jnp.float32)  61.9 us
    all_to_all x2, blocking collectives, local(): pieces = lax.all_to_all(copies, 'sub', 1, 1, tiled=True)  60.7 us
    ppermute x12, starting transfers between devices, shifted(): lax.ppermute(array, axis, [(i, (i + by) % peers) for i in range(peers)])  57.3 us
    ppermute x12, starting transfers between devices, from_behind(): lax.ppermute(value, axis, [(source, source + steps) for source in range(f...  35.5 us
    gather x6, local copies, waits for them, and re-layouts, assemble(): values[:, one_index] * one_mask[None, :]  27.9 us
    unnamed x1, blocking collectives  23.1 us
    scatter-add x6, other arithmetic, assemble(): values = values.at[:, face_index[1]].add(from_prev)  22 us
  transfers between devices with their start and end apart: 25, of which 0 were waited for; matrix products, arithmetic and copies ran while one was open for 13% of the time, Pallas kernels for 0%

profile of v1, /device:TPU:1, one launch (start us, length us, event | category | flops | bytes accessed | tf_op | source)
XLA Modules:
  0.0 573.7 jit_solution(7661381654356379550)
XLA Ops:
  1.5 11.3 %fusion.10 = f32[192,1152]{0,1:T(8,128)S(1)} fusion(f32[1,1,1152,1152]{3,2,1,0:T(8,128)} %param.10, f32[1,1,192,1152]{3,2,1,0:T(8,128)} %param.19), kind=kOutput, calls=%fused_computation.46 | convolution fusion | flops 3057647616 | bytes 7077888 | tf_op jit(solution)/shard_map/dot_general | solution.py:22
  12.8 4.7 gather_fusion
  23.9 4.0 collective-permute-start.3
  64.4 12.5 %all-to-all-start = ((f32[192,32,24]{0,2,1:T(8,128)}), f32[192,32,24]{0,2,1:T(8,128)S(1)}, u32[]{:S(2)}, u32[]{:S(2)}) async-start(f32[192,32,24]{0,2,1:T(8,128)} %bitcast.23), calls=%async_computation | async-start | bytes 1572864 | tf_op jit(solution)/shard_map/all_to_all | solution.py:76
  78.3 23.1 %all-reduce = s32[768]{0:T(1024)S(1)} all-reduce(s32[768]{0:T(1024)S(1)} %bitcast_dynamic-update-slice_fusion), channel_id=1, replica_groups=mesh['grp'=8,'sub'=32] {'sub'}, use_global_device_ids=true, to_apply=%add | all-reduce | flops 768 | bytes 6144
  101.5 5.7 scatter_custom_fusion.4
  107.7 37.2 %all_gather.13 = f32[192,768]{0,1:T(8,128)S(1)} all-gather(f32[192,24]{0,1:T(8,128)S(1)} %fusion.110), channel_id=1, replica_groups=mesh['grp'=8,'sub'=32] {'sub'}, dimensions={1}, use_global_device_ids=true | all-gather | bytes 608256 | tf_op jit(solution)/shard_map/all_gather | solution.py:79
  147.7 8.0 %bitcast_add_fusion = (f32[192,1152]{1,0:T(8,128)}, f32[192,1152]{1,0:T(8,128)}) fusion(f32[1,1,192,1152]{3,2,1,0:T(8,128)S(1)} %copy-done.6, f32[1152]{0:T(1024)} %copy-done.10, f32[192,1152]{1,0:T(8,128)S(1)} %fusion.103, f32[1,1,1152,1152]{3,2,1,0:T(8,128)} %param.11, f32[192,1152]{1,0:T(8,128)S(1)} %copy.31, f32[1,1,192,1152]{3,2,1,0:T(8,128)S(1)} %copy-done.1), kind=kOutput, calls=%fused_computation.66 | convolution fusion | flops 3058753536 | bytes 10621440 | tf_op jit(solution)/shard_map/dot_general | solution.py:22
  157.3 4.7 gather_fusion.2
  164.7 15.9 %collective-permute-start.4 = (f32[192,384]{0,1:T(8,128)}, f32[192,384]{0,1:T(8,128)}, u32[]{:S(2)}, u32[]{:S(2)}) collective-permute-start(f32[192,384]{0,1:T(8,128)} %get-tuple-element.28), channel_id=1, source_target_pairs={{0,224},{32,0},{64,32},{96,64},{128,96},{160,128},{192,160},{224,1... | collective-permute-start | bytes 884744 | tf_op jit(solution)/shard_map/ppermute | solution.py:12
  183.2 4.7 collective-permute-start.7
  202.8 11.1 %fusion.8 = f32[192,1152]{0,1:T(8,128)S(1)} fusion(f32[192,1152]{0,1:T(8,128)S(1)} %scatter_custom_fusion.8, f32[1,1,1152,1152]{3,2,1,0:T(8,128)} %param.10), kind=kOutput, calls=%fused_computation.44 | convolution fusion | flops 3057647616 | bytes 7077888 | tf_op jit(solution)/shard_map/dot_general | solution.py:22
  213.9 4.7 gather_fusion.3
  224.3 4.8 collective-permute-start.11
  247.4 30.0 %all_to_all.36 = f32[192,32,24]{0,2,1:T(8,128)} all-to-all(f32[192,32,24]{0,2,1:T(8,128)S(1)} %bitcast.271), channel_id=1, replica_groups=mesh['grp'=8,'sub'=32] {'sub'}, dimensions={1} | all-to-all | bytes 1179648 | tf_op jit(solution)/shard_map/all_to_all | solution.py:76
  277.5 6.2 %scatter_custom_fusion.13 = f32[192,768]{0,1:T(8,128)S(1)} fusion(s32[768]{0:T(1024)} %copy-done.19, f32[768,192]{1,0:T(8,128)} %bitcast.275, f32[]{:T(128)} %constant.8.clone.1), kind=kCustom, calls=%fused_computation.142 | custom fusion | bytes 590336 | tf_op jit(solution)/shard_map/scatter | solution.py:77
  284.2 42.8 %all_gather.14 = f32[192,768]{0,1:T(8,128)} all-gather(f32[192,24]{0,1:T(8,128)S(1)} %fusion.108), channel_id=1, replica_groups=mesh['grp'=8,'sub'=32] {'sub'}, dimensions={1}, use_global_device_ids=true | all-gather | bytes 608256 | tf_op jit(solution)/shard_map/all_gather | solution.py:79
  329.6 7.7 %fusion.24 = f32[192,1152]{1,0:T(8,128)} fusion(f32[192,1152]{1,0:T(8,128)S(1)} %fusion.100, f32[1,1,1152,1152]{3,2,1,0:T(8,128)} %param.11, f32[1152]{0:T(1024)S(1)} %copy-done.11, f32[192,1152]{1,0:T(8,128)S(1)} %copy-done.3, f32[1,1,192,1152]{3,2,1,0:T(8,128)S(1)} %copy-done.1), kind=kOutput, calls=%fused_computation.52 | convolution fusion | flops 3058532352 | bytes 8851968 | tf_op jit(solution)/shard_map/dot_general | solution.py:22
  338.9 4.7 gather_fusion.5
  346.4 15.2 %collective-permute-start.12 = (f32[192,384]{0,1:T(8,128)}, f32[192,384]{0,1:T(8,128)}, u32[]{:S(2)}, u32[]{:S(2)}) collective-permute-start(f32[192,384]{0,1:T(8,128)} %get-tuple-element.20), channel_id=1, source_target_pairs={{0,224},{32,0},{64,32},{96,64},{128,96},{160,128},{192,160},{224,1... | collective-permute-start | bytes 884744 | tf_op jit(solution)/shard_map/ppermute | solution.py:12
  365.4 4.7 collective-permute-start.15
  389.6 11.1 %fusion.6 = f32[192,1152]{0,1:T(8,128)S(1)} fusion(f32[192,1152]{0,1:T(8,128)S(1)} %scatter_custom_fusion.17, f32[1,1,1152,1152]{3,2,1,0:T(8,128)} %param.10), kind=kOutput, calls=%fused_computation.42 | convolution fusion | flops 3057647616 | bytes 7077888 | tf_op jit(solution)/shard_map/dot_general | solution.py:22
  400.8 4.7 gather_fusion.6
  411.2 4.8 collective-permute-start.19
  434.3 30.7 %all_to_all.37 = f32[192,32,24]{0,2,1:T(8,128)} all-to-all(f32[192,32,24]{0,2,1:T(8,128)S(1)} %bitcast.272), channel_id=1, replica_groups=mesh['grp'=8,'sub'=32] {'sub'}, dimensions={1} | all-to-all | bytes 1179648 | tf_op jit(solution)/shard_map/all_to_all | solution.py:76
  464.9 6.2 %scatter_custom_fusion.22 = f32[192,768]{0,1:T(8,128)S(1)} fusion(s32[768]{0:T(1024)} %copy-done.19, f32[768,192]{1,0:T(8,128)} %bitcast.274, f32[]{:T(128)} %constant.8.clone.1), kind=kCustom, calls=%fused_computation.140 | custom fusion | bytes 590336 | tf_op jit(solution)/shard_map/scatter | solution.py:77
  471.6 41.9 %all_gather.15 = f32[192,768]{0,1:T(8,128)} all-gather(f32[192,24]{0,1:T(8,128)S(1)} %fusion.106), channel_id=1, replica_groups=mesh['grp'=8,'sub'=32] {'sub'}, dimensions={1}, use_global_device_ids=true | all-gather | bytes 608256 | tf_op jit(solution)/shard_map/all_gather | solution.py:79
  516.2 7.7 %fusion.21 = f32[192,1152]{1,0:T(8,128)} fusion(f32[192,1152]{1,0:T(8,128)S(1)} %fusion.97, f32[1,1,1152,1152]{3,2,1,0:T(8,128)} %param.11, f32[1152]{0:T(1024)S(1)} %copy-done.11, f32[192,1152]{1,0:T(8,128)S(1)} %copy-done.2, f32[1,1,192,1152]{3,2,1,0:T(8,128)S(1)} %copy-done.1), kind=kOutput, calls=%fused_computation.51 | convolution fusion | flops 3058532352 | bytes 8851968 | tf_op jit(solution)/shard_map/dot_general | solution.py:22
  525.4 4.7 gather_fusion.8
  532.8 14.7 %collective-permute-start.20 = (f32[192,384]{0,1:T(8,128)}, f32[192,384]{0,1:T(8,128)}, u32[]{:S(2)}, u32[]{:S(2)}) collective-permute-start(f32[192,384]{0,1:T(8,128)} %get-tuple-element.12), channel_id=1, source_target_pairs={{0,224},{32,0},{64,32},{96,64},{128,96},{160,128},{192,160},{224,1... | collective-permute-start | bytes 884744 | tf_op jit(solution)/shard_map/ppermute | solution.py:12
  549.8 4.7 collective-permute-start.23
  564.6 4.0 scatter_custom_fusion.25
  (258 shorter events, 172.5 us)
Async XLA Ops:
  0.0 43.2 %copy-start = (f32[1,1,24,1152]{3,2,1,0:T(8,128)S(1)}, f32[1,1,24,1152]{3,2,1,0:T(8,128)}, u32[]{:S(2)}) copy-start(f32[1,1,24,1152]{3,2,1,0:T(8,128)} %param.12) | copy-start | bytes 331780
  19.3 8.7 %collective-permute-start = (f32[192,384]{0,1:T(8,128)S(1)}, f32[192,384]{0,1:T(8,128)S(1)}, u32[]{:S(2)}, u32[]{:S(2)}) collective-permute-start(f32[192,384]{0,1:T(8,128)S(1)} %get-tuple-element.32), channel_id=1, source_target_pairs={{0,224},{32,0},{64,32},{96,64},{128,96},{160,128},{192,160},{224,1... | collective-permute-start | bytes 884744 | tf_op jit(solution)/shard_map/ppermute | solution.py:12
  22.6 9.8 %collective-permute-start.1 = (f32[192,384]{0,1:T(8,128)S(1)}, f32[192,384]{0,1:T(8,128)}, u32[]{:S(2)}, u32[]{:S(2)}) collective-permute-start(f32[192,384]{0,1:T(8,128)S(1)} %get-tuple-element.31), channel_id=1, source_target_pairs={{0,32},{32,64},{64,96},{96,128},{128,160},{160,192},{192,224},{224... | collective-permute-start | bytes 884744 | tf_op jit(solution)/shard_map/ppermute | solution.py:12
  22.6 13.5 %collective-permute-start.2 = (f32[192,384]{0,1:T(8,128)S(1)}, f32[192,384]{0,1:T(8,128)}, u32[]{:S(2)}, u32[]{:S(2)}) collective-permute-start(f32[192,384]{0,1:T(8,128)S(1)} %get-tuple-element.30), channel_id=1, source_target_pairs={{1,0},{2,1},{3,2},{4,3},{5,4},{6,5},{7,6},{8,7},{9,8},{10,9},{11,1... | collective-permute-start | bytes 884744 | tf_op jit(solution)/shard_map/ppermute | solution.py:18
  23.9 15.8 %collective-permute-start.3 = (f32[192,384]{0,1:T(8,128)S(1)}, f32[192,384]{0,1:T(8,128)S(1)}, u32[]{:S(2)}, u32[]{:S(2)}) collective-permute-start(f32[192,384]{0,1:T(8,128)S(1)} %get-tuple-element.29), channel_id=1, source_target_pairs={{0,1},{1,2},{2,3},{3,4},{4,5},{5,6},{6,7},{7,8},{8,9},{9,10},{10,1... | collective-permute-start | bytes 884744 | tf_op jit(solution)/shard_map/ppermute | solution.py:18
  64.4 42.8 %copy-start.8 = (f32[1,768,24]{1,2,0:T(8,128)S(1)}, f32[1,768,24]{1,2,0:T(8,128)}, u32[]{:S(2)}) copy-start(f32[1,768,24]{1,2,0:T(8,128)} %param.13) | copy-start | bytes 221188
  64.4 37.0 %all-to-all-start = ((f32[192,32,24]{0,2,1:T(8,128)}), f32[192,32,24]{0,2,1:T(8,128)S(1)}, u32[]{:S(2)}, u32[]{:S(2)}) async-start(f32[192,32,24]{0,2,1:T(8,128)} %bitcast.23), calls=%async_computation | async-start | bytes 1572864 | tf_op jit(solution)/shard_map/all_to_all | solution.py:76
  107.7 40.0 %copy-start.6 = (f32[1,1,192,1152]{3,2,1,0:T(8,128)S(1)}, f32[1,1,192,1152]{3,2,1,0:T(8,128)}, u32[]{:S(2)}) copy-start(f32[1,1,192,1152]{3,2,1,0:T(8,128)} %param.19) | copy-start | bytes 2654212
  164.7 23.6 %collective-permute-start.4 = (f32[192,384]{0,1:T(8,128)}, f32[192,384]{0,1:T(8,128)}, u32[]{:S(2)}, u32[]{:S(2)}) collective-permute-start(f32[192,384]{0,1:T(8,128)} %get-tuple-element.28), channel_id=1, source_target_pairs={{0,224},{32,0},{64,32},{96,64},{128,96},{160,128},{192,160},{224,1... | collective-permute-start | bytes 884744 | tf_op jit(solution)/shard_map/ppermute | solution.py:12
  180.6 11.3 %collective-permute-start.5 = (f32[192,384]{0,1:T(8,128)}, f32[192,384]{0,1:T(8,128)}, u32[]{:S(2)}, u32[]{:S(2)}) collective-permute-start(f32[192,384]{0,1:T(8,128)} %get-tuple-element.27), channel_id=1, source_target_pairs={{0,32},{32,64},{64,96},{96,128},{128,160},{160,192},{192,224},{224... | collective-permute-start | bytes 884744 | tf_op jit(solution)/shard_map/ppermute | solution.py:12
  181.9 13.6 %collective-permute-start.6 = (f32[192,384]{0,1:T(8,128)}, f32[192,384]{0,1:T(8,128)}, u32[]{:S(2)}, u32[]{:S(2)}) collective-permute-start(f32[192,384]{0,1:T(8,128)} %get-tuple-element.26), channel_id=1, source_target_pairs={{1,0},{2,1},{3,2},{4,3},{5,4},{6,5},{7,6},{8,7},{9,8},{10,9},{11,1... | collective-permute-start | bytes 884744 | tf_op jit(solution)/shard_map/ppermute | solution.py:18
  183.2 15.9 %collective-permute-start.7 = (f32[192,384]{0,1:T(8,128)S(1)}, f32[192,384]{0,1:T(8,128)}, u32[]{:S(2)}, u32[]{:S(2)}) collective-permute-start(f32[192,384]{0,1:T(8,128)S(1)} %get-tuple-element.25), channel_id=1, source_target_pairs={{0,1},{1,2},{2,3},{3,4},{4,5},{5,6},{6,7},{7,8},{8,9},{9,10},{10,1... | collective-permute-start | bytes 884744 | tf_op jit(solution)/shard_map/ppermute | solution.py:18
  221.3 7.8 %collective-permute-start.8 = (f32[192,384]{0,1:T(8,128)S(1)}, f32[192,384]{0,1:T(8,128)}, u32[]{:S(2)}, u32[]{:S(2)}) collective-permute-start(f32[192,384]{0,1:T(8,128)S(1)} %get-tuple-element.24), channel_id=1, source_target_pairs={{0,224},{32,0},{64,32},{96,64},{128,96},{160,128},{192,160},{224,1... | collective-permute-start | bytes 884744 | tf_op jit(solution)/shard_map/ppermute | solution.py:12
  221.3 11.4 %collective-permute-start.9 = (f32[192,384]{0,1:T(8,128)}, f32[192,384]{0,1:T(8,128)}, u32[]{:S(2)}, u32[]{:S(2)}) collective-permute-start(f32[192,384]{0,1:T(8,128)} %get-tuple-element.23), channel_id=1, source_target_pairs={{0,32},{32,64},{64,96},{96,128},{128,160},{160,192},{192,224},{224... | collective-permute-start | bytes 884744 | tf_op jit(solution)/shard_map/ppermute | solution.py:12
  223.0 13.4 %collective-permute-start.10 = (f32[192,384]{0,1:T(8,128)}, f32[192,384]{0,1:T(8,128)}, u32[]{:S(2)}, u32[]{:S(2)}) collective-permute-start(f32[192,384]{0,1:T(8,128)} %get-tuple-element.22), channel_id=1, source_target_pairs={{1,0},{2,1},{3,2},{4,3},{5,4},{6,5},{7,6},{8,7},{9,8},{10,9},{11,1... | collective-permute-start | bytes 884744 | tf_op jit(solution)/shard_map/ppermute | solution.py:18
  224.3 15.7 %collective-permute-start.11 = (f32[192,384]{0,1:T(8,128)}, f32[192,384]{0,1:T(8,128)}, u32[]{:S(2)}, u32[]{:S(2)}) collective-permute-start(f32[192,384]{0,1:T(8,128)} %get-tuple-element.21), channel_id=1, source_target_pairs={{0,1},{1,2},{2,3},{3,4},{4,5},{5,6},{6,7},{7,8},{8,9},{9,10},{10,1... | collective-permute-start | bytes 884744 | tf_op jit(solution)/shard_map/ppermute | solution.py:18
  247.4 36.3 %copy-start.9 = (f32[1,768,24]{1,2,0:T(8,128)S(1)}, f32[1,768,24]{1,2,0:T(8,128)}, u32[]{:S(2)}) copy-start(f32[1,768,24]{1,2,0:T(8,128)} %param.13) | copy-start | bytes 221188
  284.2 45.5 %copy-start.3 = (f32[192,1152]{1,0:T(8,128)S(1)}, f32[192,1152]{1,0:T(8,128)}, u32[]{:S(2)}) copy-start(f32[192,1152]{1,0:T(8,128)} %copy.36) | copy-start | bytes 2654212
  346.4 25.0 %copy-start.5 = (f32[192,1152]{1,0:T(8,128)S(1)}, f32[192,1152]{1,0:T(8,128)}, u32[]{:S(2)}) copy-start(f32[192,1152]{1,0:T(8,128)} %fusion.24) | copy-start | bytes 2654212
  346.4 28.7 %collective-permute-start.12 = (f32[192,384]{0,1:T(8,128)}, f32[192,384]{0,1:T(8,128)}, u32[]{:S(2)}, u32[]{:S(2)}) collective-permute-start(f32[192,384]{0,1:T(8,128)} %get-tuple-element.20), channel_id=1, source_target_pairs={{0,224},{32,0},{64,32},{96,64},{128,96},{160,128},{192,160},{224,1... | collective-permute-start | bytes 884744 | tf_op jit(solution)/shard_map/ppermute | solution.py:12
  361.6 17.1 %collective-permute-start.13 = (f32[192,384]{0,1:T(8,128)}, f32[192,384]{0,1:T(8,128)}, u32[]{:S(2)}, u32[]{:S(2)}) collective-permute-start(f32[192,384]{0,1:T(8,128)} %get-tuple-element.19), channel_id=1, source_target_pairs={{0,32},{32,64},{64,96},{96,128},{128,160},{160,192},{192,224},{224... | collective-permute-start | bytes 884744 | tf_op jit(solution)/shard_map/ppermute | solution.py:12
  364.1 18.2 %collective-permute-start.14 = (f32[192,384]{0,1:T(8,128)}, f32[192,384]{0,1:T(8,128)}, u32[]{:S(2)}, u32[]{:S(2)}) collective-permute-start(f32[192,384]{0,1:T(8,128)} %get-tuple-element.18), channel_id=1, source_target_pairs={{1,0},{2,1},{3,2},{4,3},{5,4},{6,5},{7,6},{8,7},{9,8},{10,9},{11,1... | collective-permute-start | bytes 884744 | tf_op jit(solution)/shard_map/ppermute | solution.py:18
  365.4 20.5 %collective-permute-start.15 = (f32[192,384]{0,1:T(8,128)}, f32[192,384]{0,1:T(8,128)}, u32[]{:S(2)}, u32[]{:S(2)}) collective-permute-start(f32[192,384]{0,1:T(8,128)} %get-tuple-element.17), channel_id=1, source_target_pairs={{0,1},{1,2},{2,3},{3,4},{4,5},{5,6},{6,7},{7,8},{8,9},{9,10},{10,1... | collective-permute-start | bytes 884744 | tf_op jit(solution)/shard_map/ppermute | solution.py:18
  408.1 7.8 %collective-permute-start.16 = (f32[192,384]{0,1:T(8,128)S(1)}, f32[192,384]{0,1:T(8,128)}, u32[]{:S(2)}, u32[]{:S(2)}) collective-permute-start(f32[192,384]{0,1:T(8,128)S(1)} %get-tuple-element.16), channel_id=1, source_target_pairs={{0,224},{32,0},{64,32},{96,64},{128,96},{160,128},{192,160},{224,1... | collective-permute-start | bytes 884744 | tf_op jit(solution)/shard_map/ppermute | solution.py:12
  408.2 11.4 %collective-permute-start.17 = (f32[192,384]{0,1:T(8,128)}, f32[192,384]{0,1:T(8,128)}, u32[]{:S(2)}, u32[]{:S(2)}) collective-permute-start(f32[192,384]{0,1:T(8,128)} %get-tuple-element.15), channel_id=1, source_target_pairs={{0,32},{32,64},{64,96},{96,128},{128,160},{160,192},{192,224},{224... | collective-permute-start | bytes 884744 | tf_op jit(solution)/shard_map/ppermute | solution.py:12
  409.9 13.4 %collective-permute-start.18 = (f32[192,384]{0,1:T(8,128)}, f32[192,384]{0,1:T(8,128)}, u32[]{:S(2)}, u32[]{:S(2)}) collective-permute-start(f32[192,384]{0,1:T(8,128)} %get-tuple-element.14), channel_id=1, source_target_pairs={{1,0},{2,1},{3,2},{4,3},{5,4},{6,5},{7,6},{8,7},{9,8},{10,9},{11,1... | collective-permute-start | bytes 884744 | tf_op jit(solution)/shard_map/ppermute | solution.py:18
  411.2 15.7 %collective-permute-start.19 = (f32[192,384]{0,1:T(8,128)}, f32[192,384]{0,1:T(8,128)}, u32[]{:S(2)}, u32[]{:S(2)}) collective-permute-start(f32[192,384]{0,1:T(8,128)} %get-tuple-element.13), channel_id=1, source_target_pairs={{0,1},{1,2},{2,3},{3,4},{4,5},{5,6},{6,7},{7,8},{8,9},{9,10},{10,1... | collective-permute-start | bytes 884744 | tf_op jit(solution)/shard_map/ppermute | solution.py:18
  471.6 44.6 %copy-start.2 = (f32[192,1152]{1,0:T(8,128)S(1)}, f32[192,1152]{1,0:T(8,128)}, u32[]{:S(2)}) copy-start(f32[192,1152]{1,0:T(8,128)} %copy.42) | copy-start | bytes 2654212
  532.8 24.7 %collective-permute-start.20 = (f32[192,384]{0,1:T(8,128)}, f32[192,384]{0,1:T(8,128)}, u32[]{:S(2)}, u32[]{:S(2)}) collective-permute-start(f32[192,384]{0,1:T(8,128)} %get-tuple-element.12), channel_id=1, source_target_pairs={{0,224},{32,0},{64,32},{96,64},{128,96},{160,128},{192,160},{224,1... | collective-permute-start | bytes 884744 | tf_op jit(solution)/shard_map/ppermute | solution.py:12
  547.5 13.5 %collective-permute-start.21 = (f32[192,384]{0,1:T(8,128)}, f32[192,384]{0,1:T(8,128)}, u32[]{:S(2)}, u32[]{:S(2)}) collective-permute-start(f32[192,384]{0,1:T(8,128)} %get-tuple-element.11), channel_id=1, source_target_pairs={{0,32},{32,64},{64,96},{96,128},{128,160},{160,192},{192,224},{224... | collective-permute-start | bytes 884744 | tf_op jit(solution)/shard_map/ppermute | solution.py:12
  548.5 16.1 %collective-permute-start.22 = (f32[192,384]{0,1:T(8,128)}, f32[192,384]{0,1:T(8,128)}, u32[]{:S(2)}, u32[]{:S(2)}) collective-permute-start(f32[192,384]{0,1:T(8,128)} %get-tuple-element.10), channel_id=1, source_target_pairs={{1,0},{2,1},{3,2},{4,3},{5,4},{6,5},{7,6},{8,7},{9,8},{10,9},{11,1... | collective-permute-start | bytes 884744 | tf_op jit(solution)/shard_map/ppermute | solution.py:18
  549.8 18.9 %collective-permute-start.23 = (f32[192,384]{0,1:T(8,128)S(1)}, f32[192,384]{0,1:T(8,128)}, u32[]{:S(2)}, u32[]{:S(2)}) collective-permute-start(f32[192,384]{0,1:T(8,128)S(1)} %get-tuple-element.9), channel_id=1, source_target_pairs={{0,1},{1,2},{2,3},{3,4},{4,5},{5,6},{6,7},{7,8},{8,9},{9,10},{10,1... | collective-permute-start | bytes 884744 | tf_op jit(solution)/shard_map/ppermute | solution.py:18
  (19 other events, 204.3 us)
